TPU v7x, 256 devices: a whole 4x4x8 slice. The times are simulated.
256 devices in a mesh: path: 32 (over y, x, core), fac: 8 (over z).
Axes of the slice: x: 4, y: 4, z: 8, core: 2. Of those that a mesh axis runs over, the one named last changes fastest.
Arguments:
- shocks: bfloat16 [4, 2048, 8192], P(None, 'path', 'fac'), may hold values from -6 to 6
- chol_factor: bfloat16 [8192, 8192], P('path', 'fac')
- factor_vol: float32 [8192], P('fac'), may hold values from 0.3 to 1.5
- trade_loading: bfloat16 [8192, 4096], P(None, 'fac'), may hold values from -0.0625 to 0.0625
- basis_loading: bfloat16 [8192, 64], replicated, may hold values from -0.0625 to 0.0625
- trade_set: int32 [4096], P('fac'), may hold values from 0 to 4095, as said below
Outputs:
- exposure: float32 [4, 2048, 4096], P(None, 'path', 'fac')
Inputs may be any that keep to these rules, and one draw needn't show every extreme that they name: Each trade belongs to a netting set of its own block: trade_set[k] // 512 equals k // 512.
All inputs are finite; a program needn't handle non-finite values.
Results may differ from a plain program's by a relative error of at most 0.0047.
Values may be sent and summed in bfloat16 or wider, within the bound.
A program may use at most 128 MiB of HBM per device.

v0:
```python
import math
import jax
import jax.numpy as jnp
from jax import lax
from jax.sharding import PartitionSpec as P

F = 8192
NSETS = 4096


def solve_step(gram, moment, basis, total_paths):
    ridged = gram + 0.01 * total_paths * jnp.eye(gram.shape[0], dtype=jnp.float32)
    factor = jnp.linalg.cholesky(ridged)
    coef = jax.scipy.linalg.cho_solve((factor, True), moment)
    predicted = jnp.dot(
        basis, coef, precision=lax.Precision.HIGHEST, preferred_element_type=jnp.float32
    )
    return jnp.maximum(predicted, 0.0)


def on_device(shocks, chol_factor, factor_vol, trade_loading, basis_loading, trade_set):
    step_count, path_count, fac_width = shocks.shape
    row_count = step_count * path_count
    flat_shocks = shocks.reshape(row_count, fac_width)
    factor_share = F // lax.axis_size("fac")
    contract_last = (((1,), (1,)), ((), ()))
    full_rows = lax.all_gather(chol_factor, "path", axis=0, tiled=True)
    increments = lax.psum_scatter(
        lax.dot_general(full_rows, flat_shocks, contract_last, preferred_element_type=jnp.float32),
        "fac",
        scatter_dimension=0,
        tiled=True,
    )
    scaled = increments.reshape(factor_share, step_count, path_count) * (
        factor_vol[:, None, None] / math.sqrt(step_count)
    )
    levels = jnp.cumsum(scaled, axis=1).astype(jnp.bfloat16).reshape(factor_share, row_count)
    basis_count = basis_loading.shape[1]
    contract_first = (((0,), (0,)), ((), ()))
    piece = lax.all_gather(levels, "fac", axis=0, tiled=True)
    trade_sum = lax.dot_general(
        piece, trade_loading, contract_first, preferred_element_type=jnp.float32
    )
    basis_sum = lax.dot_general(
        piece, basis_loading, contract_first, preferred_element_type=jnp.float32
    )
    values = jax.nn.softplus(trade_sum) - 1.0
    sets_here = NSETS // lax.axis_size("fac")
    local_set = trade_set % sets_here
    member = (local_set[:, None] == jnp.arange(sets_here, dtype=jnp.int32)[None, :]).astype(
        jnp.float32
    )
    netting = jnp.dot(
        values, member, precision=lax.Precision.HIGHEST, preferred_element_type=jnp.float32
    )
    basis = jnp.tanh(basis_sum).reshape(step_count, path_count, basis_count)
    netting = netting.reshape(step_count, path_count, sets_here)
    gram = jnp.einsum(
        "tpm,tpn->tmn",
        basis,
        basis,
        precision=lax.Precision.HIGHEST,
        preferred_element_type=jnp.float32,
    )
    moment = jnp.einsum(
        "tpm,tpn->tmn",
        basis,
        netting,
        precision=lax.Precision.HIGHEST,
        preferred_element_type=jnp.float32,
    )
    total_paths = path_count * lax.axis_size("path")
    results = []
    for step in range(step_count):
        gram_total, moment_total = lax.psum((gram[step], moment[step]), "path")
        results.append(solve_step(gram_total, moment_total, basis[step], total_paths))
    return jnp.stack(results)


def solution(mesh):
    in_specs = (P(None, "path", "fac"), P("path", "fac"), P("fac"), P(None, "fac"), P(), P("fac"))
    out_specs = P(None, "path", "fac")
    return jax.shard_map(
        on_device, mesh=mesh, in_specs=in_specs, out_specs=out_specs, check_vma=False
    )
```

profile of v0, /device:TPU:6, one launch (start us, length us, event | category | flops | bytes accessed | tf_op | source)
XLA Modules:
  0.0 512.1 jit_solution(6052345440305277966)
XLA Ops:
  6.5 0.7 all-gather.3.cloned.1.call-update
  7.3 83.1 %all-gather.3.cloned.1.call-done = bf16[8192,1024]{1,0:T(8,128)(2,1)} async-done(((bf16[256,1024]{1,0:T(8,128)(2,1)}), bf16[8192,1024]{1,0:T(8,128)(2,1)}) %all-gather.3.cloned.1.call-update) | async-done | bytes 16777232 | tf_op jit(solution)/shard_map/all_gather | solution.py:27
  90.4 13.6 %fusion.53 = f32[8192,256]{1,0:T(8,128)} fusion(bf16[8192,1024]{1,0:T(8,128)(2,1)} %all-gather.3.cloned.1.call-done, bf16[256,1024]{1,0:T(8,128)(2,1)} %bitcast.96), kind=kOutput, calls=%fused_computation.96 | convolution fusion | flops 4294967296 | bytes 25690112 | tf_op jit(solution)/shard_map/dot_general | solution.py:29
  104.7 94.0 %reduce-scatter.2.cloned.1.call-done = f32[1024,256]{1,0:T(8,128)} async-done(((f32[8192,256]{1,0:T(8,128)}), f32[1024,256]{1,0:T(8,128)}) %reduce-scatter.2.cloned.1.call-update) | async-done | bytes 1048592 | tf_op jit(solution)/shard_map/reduce_scatter | solution.py:28
  198.6 1.6 copy.18
  200.2 0.9 reduce-window_convert_fusion
  201.2 53.5 %all-gather.5.cloned.1.call-done = bf16[8192,256]{0,1:T(8,128)(2,1)} async-done(((bf16[1024,256]{0,1:T(8,128)(2,1)}), bf16[8192,256]{0,1:T(8,128)(2,1)}) %all-gather.5.cloned.1.call-update) | async-done | bytes 4194320 | tf_op jit(solution)/shard_map/all_gather | solution.py:40
  254.7 3.6 convolution_tanh_fusion
  258.7 7.0 %fusion.54 = f32[256,512]{1,0:T(8,128)S(1)} fusion(bf16[8192,256]{0,1:T(8,128)(2,1)} %all-gather.5.cloned.1.call-done, bf16[8192,512]{1,0:T(8,128)(2,1)} %param.12), kind=kOutput, calls=%fused_computation.97 | convolution fusion | flops 2147483648 | bytes 13107200 | tf_op jit(solution)/shard_map/dot_general | solution.py:41
  265.7 1.0 fusion.5
  268.2 0.8 slice_bitcast_fusion.3
  269.0 110.1 %all-reduce.5.cloned.1.call-done = (f32[64,64]{0,1:T(8,128)}, f32[64,64]{0,1:T(8,128)}, f32[64,64]{0,1:T(8,128)}, f32[64,64]{0,1:T(8,128)}) async-done(((f32[64,64]{0,1:T(8,128)}, f32[64,64]{0,1:T(8,128)}, f32[64,64]{0,1:T(8,128)}, f32[64,64]{0,1:T(8,128)}), (f32[64,64]{0,1:T(8,128)}, f32[64,64]{0,1:T(8,128)}, f32[64,64]{0,1:T(8,128)}, f32[64,64]{0,1:T(8,128)})) %all-reduce.5.cloned.1.call-update) | async-done | bytes 65552 | tf_op jit(solution)/shard_map/psum | solution.py:75
  379.1 0.8 select_add_fusion
  380.0 0.8 fusion.34
  380.8 5.8 %cholesky.107 = f32[64,64]{1,0:T(8,128)S(1)} custom-call(f32[64,64]{1,0:T(8,128)S(1)} %fusion.34), custom_call_target="Cholesky" | custom-call | tf_op jit(solution)/shard_map/jit(cholesky)/cholesky | solution.py:13
  387.9 0.8 fusion.39
  388.7 5.8 %cholesky.96 = f32[64,64]{1,0:T(8,128)S(1)} custom-call(f32[64,64]{1,0:T(8,128)S(1)} %fusion.39), custom_call_target="Cholesky" | custom-call | tf_op jit(solution)/shard_map/jit(cholesky)/cholesky | solution.py:13
  396.0 0.8 select_add_fusion.2
  396.9 0.8 fusion.44
  397.7 5.8 %cholesky.85 = f32[64,64]{1,0:T(8,128)S(1)} custom-call(f32[64,64]{1,0:T(8,128)S(1)} %fusion.44), custom_call_target="Cholesky" | custom-call | tf_op jit(solution)/shard_map/jit(cholesky)/cholesky | solution.py:13
  404.9 0.8 fusion.49
  405.7 5.8 %cholesky.74 = f32[64,64]{1,0:T(8,128)S(1)} custom-call(f32[64,64]{1,0:T(8,128)S(1)} %fusion.49), custom_call_target="Cholesky" | custom-call | tf_op jit(solution)/shard_map/jit(cholesky)/cholesky | solution.py:13
  412.3 4.9 custom-call.13
  417.2 4.9 custom-call.12
  422.1 4.9 custom-call.11
  427.6 4.9 custom-call.10
  432.5 64.7 %all-reduce.7.cloned.1.call-done = (f32[64,512]{1,0:T(8,128)}, f32[64,512]{1,0:T(8,128)}, f32[64,512]{1,0:T(8,128)}, f32[64,512]{1,0:T(8,128)}) async-done(((f32[64,512]{1,0:T(8,128)}, f32[64,512]{1,0:T(8,128)}, f32[64,512]{1,0:T(8,128)}, f32[64,512]{1,0:T(8,128)}), (f32[64,512]{1,0:T(8,128)}, f32[64,512]{1,0:T(8,128)}, f32[64,512]{1,0:T(8,128)}, f32[64,512]{1,0:T(8,128)})) %all-reduce.7.cloned.1.call-update) | async-done | bytes 524304 | tf_op jit(solution)/shard_map/psum | solution.py:75
  497.3 1.2 fusion.32
  499.2 1.2 fusion.37
  501.0 1.2 fusion.42
  502.9 1.2 fusion.47
  504.7 0.8 pad_maximum_fusion
  (45 shorter events, 10.8 us)
Async XLA Ops:
  6.5 248.1 %copy-start = (bf16[8192,64]{0,1:T(8,128)(2,1)S(1)}, bf16[8192,64]{0,1:T(8,128)(2,1)}, u32[]{:S(2)}) copy-start(bf16[8192,64]{0,1:T(8,128)(2,1)} %param.13) | copy-start | bytes 3145732
  6.5 83.8 %all-gather.3.cloned.1.call-start = ((), (), s32[]{:S(2)}) async-start(), calls=%async_computation.1 | async-start | bytes 17301504 | tf_op jit(solution)/shard_map/all_gather | solution.py:27
  7.3 191.4 %reduce-scatter.2.cloned.1.call-start = ((), (), s32[]{:S(2)}) async-start(), calls=%async_computation.2 | async-start | bytes 9437184 | tf_op jit(solution)/shard_map/reduce_scatter | solution.py:28
  104.0 0.7 copy-start.1
  104.0 97.2 %copy-start.2 = (s32[512]{0:T(512)S(1)}, s32[512]{0:T(512)}, u32[]{:S(2)}) copy-start(s32[512]{0:T(512)} %param.14) | copy-start | bytes 6148
  104.0 150.7 %all-gather.5.cloned.1.call-start = ((), (), s32[]{:S(2)}) async-start(), calls=%async_computation.3 | async-start | bytes 4718592 | tf_op jit(solution)/shard_map/all_gather | solution.py:40
  201.1 178.0 %all-reduce.5.cloned.1.call-start = ((), (), s32[]{:S(2)}) async-start(), calls=%async_computation.4 | async-start | bytes 262144 | tf_op jit(solution)/shard_map/psum | solution.py:75
  268.0 229.3 %all-reduce.7.cloned.1.call-start = ((), (), s32[]{:S(2)}) async-start(), calls=%async_computation.5 | async-start | bytes 1048576 | tf_op jit(solution)/shard_map/psum | solution.py:75
Sparse Core Ops, SparseCore 0:
  9.9 80.4 all-gather.2
  104.1 94.4 reduce-scatter.1
  201.2 53.3 all-gather.4
  268.1 111.0 all-reduce.4
  382.4 114.8 all-reduce.6
where the time goes:
time: 513 us; the launch traced here: 512 us
  waiting for transfers between devices  406 us (79%)
  other arithmetic  54.8 us (11%)
  matrix products  33.4 us (7%)
  between operations  13.4 us (3%)
    psum x2, waiting for transfers between devices, on_device(): gram_total, moment_total = lax.psum((gram[step], moment[step]), 'path')  175 us
    reduce_scatter x1, waiting for transfers between devices, on_device(): lax.psum_scatter(lax.dot_general(full_rows, flat_shocks, contract_last, p...  94 us
    all_gather x1, waiting for transfers between devices, on_device(): full_rows = lax.all_gather(chol_factor, 'path', axis=0, tiled=True)  83.1 us
    all_gather x1, waiting for transfers between devices, on_device(): piece = lax.all_gather(levels, 'fac', axis=0, tiled=True)  53.5 us
    another operation x12, other arithmetic, solve_step(): factor = jnp.linalg.cholesky(ridged)  26.2 us
    another operation x8, other arithmetic, solve_step(): coef = jax.scipy.linalg.cho_solve((factor, True), moment)  22.1 us
    dot_general x1, matrix products, on_device(): lax.dot_general(full_rows, flat_shocks, contract_last, preferred_element_...  13.6 us
  transfers between devices with their start and end apart: 5, of which 5 were waited for; matrix products, arithmetic and copies ran while one was open for 11% of the time, Pallas kernels for 0%

commit v1 on v0

--- a/solution.py
+++ b/solution.py
@@ -24,7 +24,9 @@
     flat_shocks = shocks.reshape(row_count, fac_width)
     factor_share = F // lax.axis_size("fac")
     contract_last = (((1,), (1,)), ((), ()))
-    full_rows = lax.all_gather(chol_factor, "path", axis=0, tiled=True)
+    full_rows = jnp.concatenate(
+        lax.all_to_all(jnp.stack([chol_factor] * lax.axis_size("path")), "path", 0, 0), axis=0
+    )
     increments = lax.psum_scatter(
         lax.dot_general(full_rows, flat_shocks, contract_last, preferred_element_type=jnp.float32),
         "fac",

time: 513 us -> 619 us (1.21)
  blocking collectives: 0 us -> 191 us
  waiting for transfers between devices: 406 us -> 324 us
  matrix products: 33.4 us -> 26.5 us
    all_to_all x0 -> x1, blocking collectives: none -> 191 us  [on_device(): lax.all_to_all(jnp.stack([chol_factor] * lax.axis_size('path')), 'path',...]
    all_gather x1 -> x0, waiting for transfers between devices: 83.1 us -> none  [on_device(): full_rows = lax.all_gather(chol_factor, 'path', axis=0, tiled=True)]
    dot_general x1, matrix products: 13.6 us -> 6.75 us  [on_device(): lax.dot_general(full_rows, flat_shocks, contract_last, preferred_element_...]
  transfers between devices with their start and end apart: 5 -> 4, of which waited for: 5 -> 4; matrix products, arithmetic and copies ran while one was open for 11% -> 9% of each run, Pallas kernels for 0% -> 0%
where the time goes in v1:
time: 619 us; the launch traced here: 618 us
  waiting for transfers between devices  324 us (52%)
  blocking collectives  191 us (31%)
  other arithmetic  54.8 us (9%)
  matrix products  26.5 us (4%)
  between operations  13.4 us (2%)
  local copies, waits for them, and re-layouts  7.75 us (1%)
    all_to_all x1, blocking collectives, on_device(): lax.all_to_all(jnp.stack([chol_factor] * lax.axis_size('path')), 'path',...  191 us
    psum x2, waiting for transfers between devices, on_device(): gram_total, moment_total = lax.psum((gram[step], moment[step]), 'path')  175 us
    reduce_scatter x1, waiting for transfers between devices, on_device(): lax.psum_scatter(lax.dot_general(full_rows, flat_shocks, contract_last, p...  96 us
    all_gather x1, waiting for transfers between devices, on_device(): piece = lax.all_gather(levels, 'fac', axis=0, tiled=True)  53.5 us
    another operation x12, other arithmetic, solve_step(): factor = jnp.linalg.cholesky(ridged)  26.2 us
    another operation x8, other arithmetic, solve_step(): coef = jax.scipy.linalg.cho_solve((factor, True), moment)  22.1 us
  transfers between devices with their start and end apart: 4, of which 4 were waited for; matrix products, arithmetic and copies ran while one was open for 9% of the time, Pallas kernels for 0%

profile of v1, /device:TPU:6, one launch (start us, length us, event | category | flops | bytes accessed | tf_op | source)
XLA Modules:
  0.0 617.7 jit_solution(14749212158695448129)
XLA Ops:
  6.5 3.7 stack.12
  10.3 190.6 %all_to_all.5 = bf16[32,256,1024]{2,1,0:T(8,128)(2,1)S(1)} all-to-all(bf16[32,256,1024]{2,1,0:T(8,128)(2,1)S(1)} %stack.12), channel_id=1, replica_groups=mesh['path'=32,'fac'=8] {'path'}, dimensions={0} | all-to-all | bytes 33554432 | tf_op jit(solution)/shard_map/all_to_all | solution.py:28
  200.9 6.7 %fusion.53 = f32[8192,256]{1,0:T(8,128)} fusion(bf16[8192,1024]{1,0:T(8,128)(2,1)S(1)} %bitcast.94, bf16[256,1024]{1,0:T(8,128)(2,1)S(1)} %bitcast.98), kind=kOutput, calls=%fused_computation.96 | convolution fusion | flops 4294967296 | bytes 25690112 | tf_op jit(solution)/shard_map/dot_general | solution.py:31
  208.4 96.0 %reduce-scatter.2.cloned.1.call-done = f32[1024,256]{1,0:T(8,128)} async-done(((f32[8192,256]{1,0:T(8,128)}), f32[1024,256]{1,0:T(8,128)}) %reduce-scatter.2.cloned.1.call-update) | async-done | bytes 1048592 | tf_op jit(solution)/shard_map/reduce_scatter | solution.py:30
  304.4 1.6 copy.18
  306.0 0.9 reduce-window_convert_fusion
  306.9 53.5 %all-gather.2.cloned.1.call-done = bf16[8192,256]{0,1:T(8,128)(2,1)} async-done(((bf16[1024,256]{0,1:T(8,128)(2,1)}), bf16[8192,256]{0,1:T(8,128)(2,1)}) %all-gather.2.cloned.1.call-update) | async-done | bytes 4194320 | tf_op jit(solution)/shard_map/all_gather | solution.py:42
  360.4 3.6 convolution_tanh_fusion
  365.1 7.0 %fusion.54 = f32[256,512]{1,0:T(8,128)S(1)} fusion(bf16[8192,256]{0,1:T(8,128)(2,1)} %all-gather.2.cloned.1.call-done, bf16[8192,512]{1,0:T(8,128)(2,1)} %param.12), kind=kOutput, calls=%fused_computation.97 | convolution fusion | flops 2147483648 | bytes 13107200 | tf_op jit(solution)/shard_map/dot_general | solution.py:43
  372.1 1.0 fusion.5
  373.9 0.8 slice_bitcast_fusion.3
  374.7 110.1 %all-reduce.5.cloned.1.call-done = (f32[64,64]{0,1:T(8,128)}, f32[64,64]{0,1:T(8,128)}, f32[64,64]{0,1:T(8,128)}, f32[64,64]{0,1:T(8,128)}) async-done(((f32[64,64]{0,1:T(8,128)}, f32[64,64]{0,1:T(8,128)}, f32[64,64]{0,1:T(8,128)}, f32[64,64]{0,1:T(8,128)}), (f32[64,64]{0,1:T(8,128)}, f32[64,64]{0,1:T(8,128)}, f32[64,64]{0,1:T(8,128)}, f32[64,64]{0,1:T(8,128)})) %all-reduce.5.cloned.1.call-update) | async-done | bytes 65552 | tf_op jit(solution)/shard_map/psum | solution.py:77
  484.9 0.8 select_add_fusion.2
  485.7 0.8 fusion.49
  486.5 5.8 cholesky.74
  493.7 0.8 fusion.44
  494.5 5.8 cholesky.85
  501.8 0.8 select_add_fusion
  502.6 0.8 fusion.39
  503.4 5.8 cholesky.96
  510.7 0.8 fusion.34
  511.5 5.8 cholesky.107
  518.0 4.9 custom-call.10
  522.9 4.9 custom-call.11
  527.8 4.9 custom-call.12
  533.4 4.9 custom-call.13
  538.3 64.6 %all-reduce.7.cloned.1.call-done = (f32[64,512]{1,0:T(8,128)}, f32[64,512]{1,0:T(8,128)}, f32[64,512]{1,0:T(8,128)}, f32[64,512]{1,0:T(8,128)}) async-done(((f32[64,512]{1,0:T(8,128)}, f32[64,512]{1,0:T(8,128)}, f32[64,512]{1,0:T(8,128)}, f32[64,512]{1,0:T(8,128)}), (f32[64,512]{1,0:T(8,128)}, f32[64,512]{1,0:T(8,128)}, f32[64,512]{1,0:T(8,128)}, f32[64,512]{1,0:T(8,128)})) %all-reduce.7.cloned.1.call-update) | async-done | bytes 524304 | tf_op jit(solution)/shard_map/psum | solution.py:77
  602.9 1.2 fusion.47
  604.7 1.2 fusion.42
  606.6 1.2 fusion.37
  608.5 1.2 fusion.32
  610.4 0.8 pad_maximum_fusion
  (46 shorter events, 10.8 us)
Async XLA Ops:
  6.5 353.9 %copy-start = (bf16[8192,64]{0,1:T(8,128)(2,1)S(1)}, bf16[8192,64]{0,1:T(8,128)(2,1)}, u32[]{:S(2)}) copy-start(bf16[8192,64]{0,1:T(8,128)(2,1)} %param.13) | copy-start | bytes 3145732
  6.5 297.9 %reduce-scatter.2.cloned.1.call-start = ((), (), s32[]{:S(2)}) async-start(), calls=%async_computation.2 | async-start | bytes 9437184 | tf_op jit(solution)/shard_map/reduce_scatter | solution.py:30
  10.3 190.6 %copy-start.3 = (bf16[4,64,1024]{2,1,0:T(8,128)(2,1)S(1)}, bf16[4,64,1024]{2,1,0:T(8,128)(2,1)}, u32[]{:S(2)}) copy-start(bf16[4,64,1024]{2,1,0:T(8,128)(2,1)} %param.9) | copy-start | bytes 1572868
  207.7 0.7 copy-start.1
  207.7 99.3 %copy-start.2 = (s32[512]{0:T(512)S(1)}, s32[512]{0:T(512)}, u32[]{:S(2)}) copy-start(s32[512]{0:T(512)} %param.14) | copy-start | bytes 6148
  207.7 152.7 %all-gather.2.cloned.1.call-start = ((), (), s32[]{:S(2)}) async-start(), calls=%async_computation.3 | async-start | bytes 4718592 | tf_op jit(solution)/shard_map/all_gather | solution.py:42
  306.9 178.0 %all-reduce.5.cloned.1.call-start = ((), (), s32[]{:S(2)}) async-start(), calls=%async_computation.4 | async-start | bytes 262144 | tf_op jit(solution)/shard_map/psum | solution.py:77
  373.7 229.2 %all-reduce.7.cloned.1.call-start = ((), (), s32[]{:S(2)}) async-start(), calls=%async_computation.5 | async-start | bytes 1048576 | tf_op jit(solution)/shard_map/psum | solution.py:77
Sparse Core Ops, SparseCore 0:
  207.8 96.5 reduce-scatter.1
  307.0 53.3 all-gather.1
  373.8 111.0 all-reduce.4
  488.1 114.7 all-reduce.6
